TPU v7x, 32 devices: a whole 2x2x4 slice. The times are simulated.
32 devices in a mesh: ctx: 8 (over y, x, core), mp: 4 (over z).
Axes of the slice: x: 2, y: 2, z: 4, core: 2. Of those that a mesh axis runs over, the one named last changes fastest.
Arguments:
- tile_embeds: bfloat16 [4, 2048, 768], P('mp', 'ctx'), may hold values from -10 to 10
- norm_gain: float32 [768], replicated, may hold values from 0.1 to 1.9
- norm_bias: float32 [768], replicated, may hold values from -3 to 3
- w_qkv: bfloat16 [768, 2304], P('mp'), may hold values from -1.5 to 1.5
- w_out: bfloat16 [768, 768], P('mp'), may hold values from -0.21875 to 0.21875
- valid_count: int32 [4], P('mp'), may hold values from 256 to 2048
Outputs:
- encoded: bfloat16 [4, 2048, 768], P('mp', 'ctx')
All inputs are finite; a program needn't handle non-finite values.
Results may differ from a plain program's by a relative error of at most 0.008.
The roundings to bfloat16 on the way count: a program that leaves them out, or rounds other values in their place, can miss the bound.
Values may be sent and summed in bfloat16 or wider, within the bound.
No kernel may reach another device: no remote copies, remote signals or barrier semaphores. Data moves between devices by JAX's collectives and lax.ppermute only.
A program may use at most 64 MiB of HBM per device.

v0:
```python
from functools import reduce
import math
import jax
import jax.numpy as jnp
from jax import lax
from jax.sharding import PartitionSpec as P

HEADS = 12
HEAD_DIM = 64
MIDDLE_DILATION = 4
SLIDE_DILATION = 16
SHARDS_PER_SEG = 4
NEG_FILL = -1e30


def as_sent(x):

    def short(part):
        return part.astype(jnp.bfloat16) if part.dtype == jnp.float32 else part

    return jax.tree.map(short, x)


def swapped(value, axis, apart):
    mask = 2**apart
    pairs = [(source, source ^ mask) for source in range(lax.axis_size(axis))]
    return lax.ppermute(value, axis, pairs)


def layer_norm(row_data, norm_gain, norm_bias):
    floats = row_data.astype(jnp.float32)
    centre = jnp.mean(floats, axis=-1, keepdims=True)
    spread = jnp.mean((floats - centre) ** 2, axis=-1, keepdims=True)
    return ((floats - centre) * lax.rsqrt(spread + 1e-05) * norm_gain + norm_bias).astype(
        jnp.bfloat16
    )


def select_rows(head_rows, dilation_rate):
    return jnp.stack(
        [
            head_rows[head_number].reshape(-1, dilation_rate, head_rows.shape[-1])[
                :, head_number % dilation_rate
            ]
            for head_number in range(head_rows.shape[0])
        ]
    )


def build_step(query_block, offsets, dilation_rate, total_valid):
    rescale_factor = 1.0 / math.sqrt(query_block.shape[-1])

    def compute(running, shard_part, first):
        running_max, running_sum, running_num = running
        key_matrix, value_matrix = shard_part
        count_here = key_matrix.shape[1]
        dilated_index = first + jnp.arange(count_here, dtype=jnp.int32)
        key_position = dilated_index[None, :] * dilation_rate + offsets[:, None]
        allowed = key_position < total_valid
        logit_matrix = (
            jnp.einsum("hqe,hke->hqk", query_block, key_matrix, preferred_element_type=jnp.float32)
            * rescale_factor
        )
        logit_matrix = jnp.where(allowed[:, None, :], logit_matrix, NEG_FILL)
        new_max = jnp.maximum(running_max, jnp.max(logit_matrix, axis=-1))
        rescale = jnp.exp(running_max - new_max)
        weights = jnp.where(allowed[:, None, :], jnp.exp(logit_matrix - new_max[..., None]), 0.0)
        running_sum = jnp.sum(weights, axis=-1)
        running_num = jnp.einsum(
            "hqk,hke->hqe",
            weights.astype(jnp.bfloat16),
            value_matrix,
            preferred_element_type=jnp.float32,
        )
        return (new_max, running_sum, running_num)

    return compute


def initial_stats(head_count, query_count, head_dim):
    return (
        jnp.full((head_count, query_count), NEG_FILL, jnp.float32),
        jnp.zeros((head_count, query_count), jnp.float32),
        jnp.zeros((head_count, query_count, head_dim), jnp.float32),
    )


def widen_rows(values, offsets, dilation_rate, fill_value):
    picked = jnp.arange(dilation_rate)[None, :] == offsets[:, None]
    if values.ndim == 2:
        return jnp.where(picked[:, None, :], values[:, :, None], fill_value).reshape(
            values.shape[0], -1
        )
    return jnp.where(picked[:, None, :, None], values[:, :, None, :], fill_value).reshape(
        values.shape[0], -1, values.shape[-1]
    )


def local(tile_embeds, norm_gain, norm_bias, w_qkv, w_out, valid_count):
    tile_rows = tile_embeds[0]
    local_rows = tile_rows.shape[0]
    model_width = tile_rows.shape[1]
    head_count = HEADS
    head_dim = HEAD_DIM
    total_valid = valid_count[0]
    device_index = lax.axis_index("ctx")
    first_row = device_index * local_rows
    normed = layer_norm(tile_rows, norm_gain, norm_bias)
    whole_qkv, whole_out = (
        lax.all_gather(w_qkv, "mp", axis=0, tiled=True),
        lax.all_gather(w_out, "mp", axis=0, tiled=True),
    )
    projected = jnp.dot(normed, whole_qkv, preferred_element_type=jnp.float32).astype(jnp.bfloat16)
    gathered_queries = (
        projected[:, :model_width].reshape(local_rows, head_count, head_dim).transpose(1, 0, 2)
    )
    gathered_keys = (
        projected[:, model_width : 2 * model_width]
        .reshape(local_rows, head_count, head_dim)
        .transpose(1, 0, 2)
    )
    gathered_values = (
        projected[:, 2 * model_width :].reshape(local_rows, head_count, head_dim).transpose(1, 0, 2)
    )
    position = first_row + jnp.arange(local_rows, dtype=jnp.int32)
    key_valid = position < total_valid
    head_shifts = jnp.arange(head_count, dtype=jnp.int32)
    local_step = build_step(gathered_queries, head_shifts * 0, 1, total_valid)
    local_stats = local_step(
        initial_stats(head_count, local_rows, head_dim), (gathered_keys, gathered_values), first_row
    )
    middle_shifts = head_shifts % MIDDLE_DILATION
    middle_queries = select_rows(gathered_queries, MIDDLE_DILATION)
    middle_keys = select_rows(gathered_keys, MIDDLE_DILATION)
    middle_values = select_rows(gathered_values, MIDDLE_DILATION)
    grouped_rows = SHARDS_PER_SEG * local_rows // MIDDLE_DILATION
    mid_step = build_step(middle_queries, middle_shifts, MIDDLE_DILATION, total_valid)
    mid_initial = initial_stats(head_count, middle_queries.shape[1], head_dim)
    gathered = (middle_keys, middle_values)
    for bit_number in range(SHARDS_PER_SEG.bit_length() - 1):
        partner = jax.tree.map(
            lambda part, own: part.astype(own.dtype),
            swapped(as_sent(gathered), "ctx", bit_number),
            gathered,
        )
        lower_half = device_index // (1 << bit_number) % 2 == 0
        gathered = tuple(
            (
                jnp.where(
                    lower_half,
                    jnp.concatenate([own_part, other_part], 1),
                    jnp.concatenate([other_part, own_part], 1),
                )
                for own_part, other_part in zip(gathered, partner)
            )
        )
    middle_state = mid_step(mid_initial, gathered, device_index // SHARDS_PER_SEG * grouped_rows)
    slide_shifts = head_shifts % SLIDE_DILATION
    slide_queries = select_rows(gathered_queries, SLIDE_DILATION)
    slide_keys = select_rows(gathered_keys, SLIDE_DILATION)
    slide_values = select_rows(gathered_values, SLIDE_DILATION)
    slide_step = build_step(slide_queries, slide_shifts, SLIDE_DILATION, total_valid)
    slide_state = slide_step(
        initial_stats(head_count, slide_queries.shape[1], head_dim),
        (
            lax.all_gather(slide_keys, "ctx", axis=1, tiled=True),
            lax.all_gather(slide_values, "ctx", axis=1, tiled=True),
        ),
        jnp.int32(0),
    )
    branches = [local_stats]
    for branch_stats, offsets, dilation_rate in (
        (middle_state, middle_shifts, MIDDLE_DILATION),
        (slide_state, slide_shifts, SLIDE_DILATION),
    ):
        branches.append(
            (
                widen_rows(branch_stats[0], offsets, dilation_rate, NEG_FILL),
                widen_rows(branch_stats[1], offsets, dilation_rate, 0.0),
                widen_rows(branch_stats[2], offsets, dilation_rate, 0.0),
            )
        )
    top_score = reduce(jnp.maximum, [entry[0] for entry in branches])
    denominator = sum((jnp.exp(entry[0] - top_score) * entry[1] for entry in branches))
    weighted_sum = sum((jnp.exp(entry[0] - top_score)[..., None] * entry[2] for entry in branches))
    head_result = jnp.where(key_valid[None, :, None], weighted_sum / denominator[..., None], 0.0)
    attention = head_result.astype(jnp.bfloat16).transpose(1, 0, 2).reshape(local_rows, model_width)
    projection = jnp.dot(attention, whole_out, preferred_element_type=jnp.float32)
    return (tile_rows.astype(jnp.float32) + projection).astype(jnp.bfloat16)[None]


def solution(mesh):
    placed = (P("mp", "ctx", None), P(), P(), P("mp", None), P("mp", None), P("mp"))
    return jax.shard_map(
        local, mesh=mesh, in_specs=placed, out_specs=P("mp", "ctx", None), check_vma=False
    )
```

profile of v0, /device:TPU:0, one launch (start us, length us, event | category | flops | bytes accessed | tf_op | source)
XLA Modules:
  0.0 249.5 jit_solution(8458888001286115925)
XLA Ops:
  13.9 67.7 %all-gather.3.cloned.1.call-done = bf16[768,2304]{1,0:T(8,128)(2,1)} async-done(((bf16[192,2304]{1,0:T(8,128)(2,1)}), bf16[768,2304]{1,0:T(8,128)(2,1)}) %all-gather.3.cloned.1.call-update) | async-done | bytes 3538960 | tf_op jit(solution)/shard_map/all_gather | solution.py:110
  81.7 3.3 %convolution_convert_fusion = bf16[256,2304]{1,0:T(8,128)(2,1)S(1)} fusion(bf16[768,2304]{1,0:T(8,128)(2,1)} %all-gather.3.cloned.1.call-done, bf16[1,256,768]{2,1,0:T(8,128)(2,1)} %param.6, f32[768]{0:T(1024)} %param.8, f32[768]{0:T(1024)} %param.7, f32[256]{0:T(256)S(1)} %add_rsqrt_fusion, f32[256]{0:T(256)S(1)} %broadcast_multiply_fusion), kind=kOutput, calls=%fused_computation | convolution fusion | flops 907739136 | bytes 5120000 | tf_op jit(solution)/shard_map/dot_general | solution.py:113
  104.9 10.6 %all_gather.13 = bf16[12,128,64]{2,1,0:T(8,128)(2,1)S(1)} all-gather(bf16[12,16,64]{2,1,0:T(8,128)(2,1)S(1)} %constant_dynamic-update-slice_fusion.36), channel_id=1, replica_groups=mesh['ctx'=8,'mp'=4] {'ctx'}, dimensions={1}, use_global_device_ids=true | all-gather | bytes 221184 | tf_op jit(solution)/shard_map/all_gather | solution.py:166
  117.5 1.8 fusion
  121.8 1.5 copy.509
  124.8 1.5 copy.511
  126.2 1.5 slice.558
  127.7 1.5 copy.513
  129.2 1.5 slice.560
  130.7 1.5 copy.515
  132.1 1.5 slice.562
  133.6 1.5 copy.517
  135.1 1.5 slice.564
  136.6 1.5 copy.519
  138.0 1.5 slice.566
  139.5 1.5 copy.521
  141.0 1.5 slice.568
  142.5 1.5 copy.523
  144.0 1.5 slice.570
  145.4 1.5 copy.525
  146.9 1.5 slice.572
  148.4 1.5 copy.527
  149.9 1.5 slice.574
  151.3 1.5 copy.529
  152.8 1.5 slice.576
  154.3 1.5 copy.531
  156.7 1.4 constant_dynamic-update-slice_fusion.58
  158.1 1.4 constant_dynamic-update-slice_fusion.57
  160.8 1.4 constant_dynamic-update-slice_fusion.55
  164.9 1.4 constant_dynamic-update-slice_fusion.52
  166.2 1.4 constant_dynamic-update-slice_fusion.51
  180.7 10.5 %all_gather.14 = bf16[12,128,64]{2,1,0:T(8,128)(2,1)S(1)} all-gather(bf16[12,16,64]{2,1,0:T(8,128)(2,1)S(1)} %constant_dynamic-update-slice_fusion.60), channel_id=1, replica_groups=mesh['ctx'=8,'mp'=4] {'ctx'}, dimensions={1}, use_global_device_ids=true | all-gather | bytes 221184 | tf_op jit(solution)/shard_map/all_gather | solution.py:167
  191.2 1.4 constant_dynamic-update-slice_fusion.10
  195.3 1.4 constant_dynamic-update-slice_fusion.7
  196.6 1.4 constant_dynamic-update-slice_fusion.6
  204.8 2.1 fusion.1
  207.8 2.1 maximum_select_fusion.4
  214.2 2.7 %copy.559 = f32[12,256,64]{1,2,0:T(8,128)} copy(f32[12,256,64]{2,1,0:T(8,128)} %bitcast.410) | data formatting | bytes 1572864 | tf_op jit(solution)/shard_map/jit(_where)/broadcast_in_dim | solution.py:94
  217.0 1.9 maximum_select_fusion.5
  218.9 1.5 collective-permute-start.3
  221.6 2.8 %fusion.78 = (f32[12,64]{1,0:T(8,128)S(1)}, f32[12,64,256]{2,1,0:T(8,128)}) fusion(bf16[12,64,64]{2,1,0:T(8,128)(2,1)} %constant_dynamic-update-slice_fusion, bf16[12,128,64]{2,1,0:T(8,128)(2,1)} %collective-permute-done.1, bf16[12,128,64]{2,1,0:T(8,128)(2,1)} %maximum_select_fusion.4, pred[]{:T(512)S(6)} %eq.109, pred[12,256]{1,0:T(8,128)(4,1)S(1)} %copy-done.12), kind=kOutput, calls=%fused_computation.238 | convolution fusion | flops 27524352 | bytes 1284097 | tf_op jit(solution)/shard_map/hqe,hke->hqk/dot_general | solution.py:61
  224.6 1.5 fusion.48
  226.3 3.9 %collective-permute-done.3 = bf16[12,128,64]{2,1,0:T(8,128)(2,1)} collective-permute-done((bf16[12,128,64]{2,1,0:T(8,128)(2,1)}, bf16[12,128,64]{2,1,0:T(8,128)(2,1)}, u32[]{:S(2)}, u32[]{:S(2)}) %collective-permute-start.3) | collective-permute-done | bytes 196640 | tf_op jit(solution)/shard_map/ppermute | solution.py:27
  230.3 2.1 fusion.40
  232.5 1.4 broadcast_in_dim.270
  233.9 2.7 %copy.534 = f32[12,256,64]{1,2,0:T(8,128)} copy(f32[12,256,64]{2,1,0:T(8,128)} %bitcast.411) | data formatting | bytes 1572864 | tf_op jit(solution)/shard_map/jit(_where)/broadcast_in_dim | solution.py:94
  236.7 3.3 %fusion.26 = bf16[12,256,64]{1,2,0:T(8,128)(2,1)} fusion(bf16[12,256,64]{1,2,0:T(8,128)(2,1)} %bitcast.417, f32[12,256,256]{1,2,0:T(8,128)S(1)} %get-tuple-element.49, f32[12,256]{1,0:T(8,128)} %broadcast_maximum_fusion, pred[256]{0:T(512)(128)(4,1)} %add_compare_fusion.2, f32[12,256,64]{1,2,0:T(8,128)} %copy.559, f32[12,256,64]{1,2,0:T(8,128)} %copy.534, ...), kind=kOutput, calls=%fused_computation.23 | convolution fusion | flops 106561536 | bytes 5572864 | tf_op jit(solution)/shard_map/hqk,hke->hqe/dot_general | solution.py:69
  240.0 2.7 %fusion.17 = bf16[1,256,768]{2,1,0:T(8,128)(2,1)} fusion(bf16[256,768]{0,1:T(8,128)(2,1)} %bitcast.420, bf16[768,768]{1,0:T(8,128)(2,1)} %all-gather.5.cloned.1.call-done, bf16[1,256,768]{2,1,0:T(8,128)(2,1)S(1)} %copy-done), kind=kOutput, calls=%fused_computation.15 | convolution fusion | flops 302579712 | bytes 2359296 | tf_op jit(solution)/shard_map/dot_general | solution.py:188
  (233 shorter events, 66.5 us)
Async XLA Ops:
  6.5 75.1 %all-gather.3.cloned.1.call-start = ((), (), s32[]{:S(2)}) async-start(), calls=%async_computation | async-start | bytes 4423680 | tf_op jit(solution)/shard_map/all_gather | solution.py:110
  7.3 232.8 %all-gather.5.cloned.1.call-start = ((), (), s32[]{:S(2)}) async-start(), calls=%async_computation.1 | async-start | bytes 1474560 | tf_op jit(solution)/shard_map/all_gather | solution.py:111
  13.4 102.5 %copy-start.10 = (pred[12,128]{1,0:T(8,128)(4,1)}, pred[12,128]{1,0:T(8,128)(4,1)S(1)}, u32[]{:S(2)}) copy-start(pred[12,128]{1,0:T(8,128)(4,1)S(1)} %add_compare_fusion.1) | copy-start | bytes 4612
  95.2 112.6 %collective-permute-start = (bf16[12,64,64]{2,1,0:T(8,128)(2,1)}, bf16[12,64,64]{2,1,0:T(8,128)(2,1)}, u32[]{:S(2)}, u32[]{:S(2)}) collective-permute-start(bf16[12,64,64]{2,1,0:T(8,128)(2,1)} %constant_dynamic-update-slice_fusion.12), channel_id=1, source_target_pairs={{0,4},{4,0},{8,12},{12,8},{16,20},{20,16},{24,28},{28,24},{1,5},{5... | collective-permute-start | bytes 294920 | tf_op jit(solution)/shard_map/ppermute | solution.py:27
  95.4 21.5 %copy-start.1 = (bf16[256,768]{0,1:T(8,128)(2,1)}, bf16[256,768]{0,1:T(8,128)(2,1)S(1)}, u32[]{:S(2)}) copy-start(bf16[256,768]{0,1:T(8,128)(2,1)S(1)} %copy.405) | copy-start | bytes 1179652
  121.0 85.9 %copy-start.2 = (bf16[256,768]{0,1:T(8,128)(2,1)}, bf16[256,768]{0,1:T(8,128)(2,1)S(1)}, u32[]{:S(2)}) copy-start(bf16[256,768]{0,1:T(8,128)(2,1)S(1)} %copy.506) | copy-start | bytes 1179652
  155.8 51.1 %copy-start.3 = (f32[12,16,128]{2,1,0:T(8,128)S(1)}, f32[12,16,128]{2,1,0:T(8,128)}, u32[]{:S(2)}) copy-start(f32[12,16,128]{2,1,0:T(8,128)} %get-tuple-element.51) | copy-start | bytes 294916
  155.8 51.1 %copy-start.5 = (f32[12,16]{1,0:T(8,128)S(1)}, f32[12,16]{1,0:T(8,128)}, u32[]{:S(2)}) copy-start(f32[12,16]{1,0:T(8,128)} %broadcast_maximum_fusion.1) | copy-start | bytes 2308
  155.8 51.1 %copy-start.11 = (pred[12,128]{1,0:T(8,128)(4,1)S(1)}, pred[12,128]{1,0:T(8,128)(4,1)}, u32[]{:S(2)}) copy-start(pred[12,128]{1,0:T(8,128)(4,1)} %copy-done.10) | copy-start | bytes 4612
  155.8 51.4 %copy-start.6 = (bf16[64,1,64]{2,1,0:T(2,128)(2,1)S(1)}, bf16[64,1,64]{2,1,0:T(2,128)(2,1)}, u32[]{:S(2)}) copy-start(bf16[64,1,64]{2,1,0:T(2,128)(2,1)} %slice.505) | copy-start | bytes 24580
  170.9 46.1 %collective-permute-start.2 = (bf16[12,64,64]{2,1,0:T(8,128)(2,1)}, bf16[12,64,64]{2,1,0:T(8,128)(2,1)}, u32[]{:S(2)}, u32[]{:S(2)}) collective-permute-start(bf16[12,64,64]{2,1,0:T(8,128)(2,1)} %constant_dynamic-update-slice_fusion.48), channel_id=1, source_target_pairs={{0,4},{4,0},{8,12},{12,8},{16,20},{20,16},{24,28},{28,24},{1,5},{5... | collective-permute-start | bytes 294920 | tf_op jit(solution)/shard_map/ppermute | solution.py:27
  206.9 10.1 %copy-start.4 = (bf16[12,64,64]{2,1,0:T(8,128)(2,1)S(1)}, bf16[12,64,64]{2,1,0:T(8,128)(2,1)}, u32[]{:S(2)}) copy-start(bf16[12,64,64]{2,1,0:T(8,128)(2,1)} %constant_dynamic-update-slice_fusion.48) | copy-start | bytes 294916
  209.9 11.7 %collective-permute-start.1 = (bf16[12,128,64]{2,1,0:T(8,128)(2,1)}, bf16[12,128,64]{2,1,0:T(8,128)(2,1)}, u32[]{:S(2)}, u32[]{:S(2)}) collective-permute-start(bf16[12,128,64]{2,1,0:T(8,128)(2,1)} %maximum_select_fusion.4), channel_id=1, source_target_pairs={{0,8},{4,12},{8,0},{12,4},{16,24},{20,28},{24,16},{28,20},{1,9},{5... | collective-permute-start | bytes 589832 | tf_op jit(solution)/shard_map/ppermute | solution.py:27
  213.0 8.7 %copy-start.12 = (pred[12,256]{1,0:T(8,128)(4,1)S(1)}, pred[12,256]{1,0:T(8,128)(4,1)}, u32[]{:S(2)}) copy-start(pred[12,256]{1,0:T(8,128)(4,1)} %add_compare_fusion) | copy-start | bytes 9220
  218.9 11.4 %collective-permute-start.3 = (bf16[12,128,64]{2,1,0:T(8,128)(2,1)}, bf16[12,128,64]{2,1,0:T(8,128)(2,1)}, u32[]{:S(2)}, u32[]{:S(2)}) collective-permute-start(bf16[12,128,64]{2,1,0:T(8,128)(2,1)} %maximum_select_fusion.5), channel_id=1, source_target_pairs={{0,8},{4,12},{8,0},{12,4},{16,24},{20,28},{24,16},{28,20},{1,9},{5... | collective-permute-start | bytes 589832 | tf_op jit(solution)/shard_map/ppermute | solution.py:27
  232.4 4.2 %copy-start.7 = (f32[12,256]{1,0:T(8,128)S(1)}, f32[12,256]{1,0:T(8,128)}, u32[]{:S(2)}) copy-start(f32[12,256]{1,0:T(8,128)} %fusion.1) | copy-start | bytes 36868
  232.4 4.2 %copy-start.8 = (f32[12,256]{1,0:T(8,128)S(1)}, f32[12,256]{1,0:T(8,128)}, u32[]{:S(2)}) copy-start(f32[12,256]{1,0:T(8,128)} %broadcast_in_dim.281) | copy-start | bytes 36868
  232.4 4.2 %copy-start.9 = (f32[12,256]{1,0:T(8,128)S(1)}, f32[12,256]{1,0:T(8,128)}, u32[]{:S(2)}) copy-start(f32[12,256]{1,0:T(8,128)} %broadcast_in_dim.266) | copy-start | bytes 36868
  232.4 4.2 %copy-start.13 = (pred[12,256]{1,0:T(8,128)(4,1)S(1)}, pred[12,256]{1,0:T(8,128)(4,1)}, u32[]{:S(2)}) copy-start(pred[12,256]{1,0:T(8,128)(4,1)} %copy.456) | copy-start | bytes 9220
  232.4 4.2 %copy-start.14 = (pred[12,256]{1,0:T(8,128)(4,1)S(1)}, pred[12,256]{1,0:T(8,128)(4,1)}, u32[]{:S(2)}) copy-start(pred[12,256]{1,0:T(8,128)(4,1)} %broadcast_in_dim.261) | copy-start | bytes 9220
  236.7 3.3 %copy-start = (bf16[1,256,768]{2,1,0:T(8,128)(2,1)S(1)}, bf16[1,256,768]{2,1,0:T(8,128)(2,1)}, u32[]{:S(2)}) copy-start(bf16[1,256,768]{2,1,0:T(8,128)(2,1)} %param.6) | copy-start | bytes 1179652
Sparse Core Ops, SparseCore 0:
  8.9 72.6 all-gather.2
  83.2 28.6 all-gather.4
where the time goes:
time: 254 us; the launch traced here: 250 us
  local copies, waits for them, and re-layouts  107 us (42%)
  waiting for transfers between devices  74.3 us (29%)
  blocking collectives  21.1 us (8%)
  matrix products  17.2 us (7%)
  between operations  14.9 us (6%)
  other arithmetic  12.8 us (5%)
    all_gather x1, waiting for transfers between devices, local(): lax.all_gather(w_qkv, 'mp', axis=0, tiled=True)  67.7 us
    slice x111, local copies, waits for them, and re-layouts, select_rows(): head_rows[head_number].reshape(-1, dilation_rate, head_rows.shape[-1])  54.9 us
    unnamed x96, local copies, waits for them, and re-layouts  35.4 us
    all_gather x1, blocking collectives, local(): lax.all_gather(slide_keys, 'ctx', axis=1, tiled=True)  10.6 us
    all_gather x1, blocking collectives, local(): lax.all_gather(slide_values, 'ctx', axis=1, tiled=True)  10.5 us
    broadcast_in_dim x4, local copies, waits for them, and re-layouts, widen_rows(): jnp.where(picked[:, None, :, None], values[:, :, None, :], fill_value)  8.16 us
    dot_general x3, matrix products, compute(): jnp.einsum('hqk,hke->hqe', weights.astype(jnp.bfloat16), value_matrix, pr...  5.71 us
    dot_general x3, matrix products, compute(): jnp.einsum('hqe,hke->hqk', query_block, key_matrix, preferred_element_typ...  5.55 us
  transfers between devices with their start and end apart: 6, of which 3 were waited for; matrix products, arithmetic and copies ran while one was open for 54% of the time, Pallas kernels for 0%

commit v1 on v0

--- a/solution.py
+++ b/solution.py
@@ -11,6 +11,16 @@
 SLIDE_DILATION = 16
 SHARDS_PER_SEG = 4
 NEG_FILL = -1e30
+
+
+def ring_gather(x, axis, dim):
+    ways, here, step = (lax.axis_size(axis), lax.axis_index(axis), x.shape[dim])
+    shape = [n * ways if d == dim else n for d, n in enumerate(x.shape)]
+    full = lax.dynamic_update_slice_in_dim(jnp.zeros(shape, x.dtype), x, here * step, axis=dim)
+    for far in range(1, ways):
+        x = lax.ppermute(x, axis, [(d, (d + 1) % ways) for d in range(ways)])
+        full = lax.dynamic_update_slice_in_dim(full, x, (here - far) % ways * step, axis=dim)
+    return full
 
 
 def as_sent(x):
@@ -164,7 +174,7 @@
         initial_stats(head_count, slide_queries.shape[1], head_dim),
         (
             lax.all_gather(slide_keys, "ctx", axis=1, tiled=True),
-            lax.all_gather(slide_values, "ctx", axis=1, tiled=True),
+            ring_gather(slide_values, "ctx", 1),
         ),
         jnp.int32(0),
     )

time: 254 us -> 309 us (1.22)
  the two profiles are of different devices: /device:TPU:0 before, /device:TPU:1 now
where the time goes in v1:
time: 309 us; the launch traced here: 304 us
  local copies, waits for them, and re-layouts  160 us (52%)
  waiting for transfers between devices  70.8 us (23%)
  matrix products  16.6 us (5%)
  starting transfers between devices  16.4 us (5%)
  between operations  15.2 us (5%)
  other arithmetic  13 us (4%)
  blocking collectives  11.9 us (4%)
    all_gather x1, waiting for transfers between devices, local(): lax.all_gather(w_qkv, 'mp', axis=0, tiled=True)  66.3 us
    slice x111, local copies, waits for them, and re-layouts, select_rows(): head_rows[head_number].reshape(-1, dilation_rate, head_rows.shape[-1])  59.2 us
    unnamed x120, local copies, waits for them, and re-layouts  41.2 us
    dynamic_update_slice x7, local copies, waits for them, and re-layouts, ring_gather(): lax.dynamic_update_slice_in_dim(full, x, (here - far) % ways * step, axis...  27 us
    all_gather x1, blocking collectives, local(): lax.all_gather(slide_keys, 'ctx', axis=1, tiled=True)  11.9 us
    ppermute x7, local copies, waits for them, and re-layouts, ring_gather(): x = lax.ppermute(x, axis, [(d, (d + 1) % ways) for d in range(ways)])  10.4 us
    ppermute x7, starting transfers between devices, ring_gather(): x = lax.ppermute(x, axis, [(d, (d + 1) % ways) for d in range(ways)])  9.87 us
    broadcast_in_dim x4, local copies, waits for them, and re-layouts, widen_rows(): jnp.where(picked[:, None, :, None], values[:, :, None, :], fill_value)  8.2 us
  transfers between devices with their start and end apart: 13, of which 4 were waited for; matrix products, arithmetic and copies ran while one was open for 62% of the time, Pallas kernels for 0%

profile of v1, /device:TPU:1, one launch (start us, length us, event | category | flops | bytes accessed | tf_op | source)
XLA Modules:
  0.0 304.1 jit_solution(15619759506395467800)
XLA Ops:
  14.7 66.3 %all-gather.3.cloned.1.call-done = bf16[768,2304]{1,0:T(8,128)(2,1)} async-done(((bf16[192,2304]{1,0:T(8,128)(2,1)}), bf16[768,2304]{1,0:T(8,128)(2,1)}) %all-gather.3.cloned.1.call-update) | async-done | bytes 3538960 | tf_op jit(solution)/shard_map/all_gather | solution.py:120
  81.0 3.3 %convolution_convert_fusion = bf16[256,2304]{1,0:T(8,128)(2,1)S(1)} fusion(bf16[768,2304]{1,0:T(8,128)(2,1)} %all-gather.3.cloned.1.call-done, bf16[1,256,768]{2,1,0:T(8,128)(2,1)} %param.6, f32[768]{0:T(1024)} %param.8, f32[768]{0:T(1024)} %param.7, f32[256]{0:T(256)S(1)} %add_rsqrt_fusion, f32[256]{0:T(256)S(1)} %broadcast_multiply_fusion), kind=kOutput, calls=%fused_computation | convolution fusion | flops 907739136 | bytes 5120000 | tf_op jit(solution)/shard_map/dot_general | solution.py:123
  105.0 11.9 %all_gather.10 = bf16[12,128,64]{2,1,0:T(8,128)(2,1)} all-gather(bf16[12,16,64]{2,1,0:T(8,128)(2,1)S(1)} %constant_dynamic-update-slice_fusion.36), channel_id=1, replica_groups=mesh['ctx'=8,'mp'=4] {'ctx'}, dimensions={1}, use_global_device_ids=true | all-gather | bytes 221184 | tf_op jit(solution)/shard_map/all_gather | solution.py:176
  124.1 1.8 fusion
  128.5 1.5 copy.523
  131.4 1.5 copy.525
  134.4 1.5 copy.527
  135.8 1.5 slice.560
  137.3 1.5 copy.529
  143.2 1.5 copy.533
  146.2 1.5 copy.535
  147.7 1.5 slice.568
  152.1 1.5 copy.539
  155.0 1.5 copy.541
  156.5 1.5 slice.574
  158.0 1.5 copy.543
  159.5 1.5 copy.545
  200.4 2.2 fusion.1
  210.1 2.3 collective-permute-start.6
  213.6 2.3 collective-permute-start.7
  215.9 2.0 collective-permute-done.7
  218.0 1.5 collective-permute-start.8
  219.7 1.6 copy.572
  221.6 2.3 collective-permute-start.2
  224.0 4.1 %dynamic_update_slice.24 = bf16[12,128,64]{1,2,0:T(8,128)(2,1)S(1)} dynamic-update-slice(bf16[12,128,64]{1,2,0:T(8,128)(2,1)S(1)} %broadcast_in_dim.278, bf16[12,16,64]{1,2,0:T(8,128)(2,1)} %copy.572, s32[]{:T(128)} %constant.140.clone.1, s32[]{:T(128)S(6)} %select_n.233, s32[]{:T(128)} %constant.140.clone.1) | dynamic-update-slice | bytes 49156 | tf_op jit(solution)/shard_map/dynamic_update_slice | solution.py:19
  228.1 1.6 copy.573
  229.7 2.5 dynamic_update_slice.25
  232.2 1.6 copy.574
  233.8 4.1 %dynamic_update_slice.26 = bf16[12,128,64]{1,2,0:T(8,128)(2,1)S(1)} dynamic-update-slice(bf16[12,128,64]{1,2,0:T(8,128)(2,1)S(1)} %dynamic_update_slice.25, bf16[12,16,64]{1,2,0:T(8,128)(2,1)} %copy.574, s32[]{:T(128)} %constant.140.clone.1, s32[]{:T(128)S(6)} %select_n.237, s32[]{:T(128)} %constant.140.clone.1) | dynamic-update-slice | bytes 49156 | tf_op jit(solution)/shard_map/dynamic_update_slice | solution.py:22
  237.9 1.6 copy.575
  239.5 4.1 %dynamic_update_slice.27 = bf16[12,128,64]{1,2,0:T(8,128)(2,1)S(1)} dynamic-update-slice(bf16[12,128,64]{1,2,0:T(8,128)(2,1)S(1)} %dynamic_update_slice.26, bf16[12,16,64]{1,2,0:T(8,128)(2,1)} %copy.575, s32[]{:T(128)} %constant.140.clone.1, s32[]{:T(128)S(6)} %select_n.239, s32[]{:T(128)} %constant.140.clone.1) | dynamic-update-slice | bytes 49156 | tf_op jit(solution)/shard_map/dynamic_update_slice | solution.py:22
  243.6 2.1 collective-permute-start.9
  245.7 2.1 maximum_select_fusion.4
  249.5 2.1 maximum_select_fusion.5
  251.6 2.2 collective-permute-start.3
  254.7 4.1 %dynamic_update_slice.28 = bf16[12,128,64]{1,2,0:T(8,128)(2,1)S(1)} dynamic-update-slice(bf16[12,128,64]{1,2,0:T(8,128)(2,1)S(1)} %dynamic_update_slice.27, bf16[12,16,64]{1,2,0:T(8,128)(2,1)} %copy.576, s32[]{:T(128)} %constant.140.clone.1, s32[]{:T(128)S(6)} %select_n.241, s32[]{:T(128)} %constant.140.clone.1) | dynamic-update-slice | bytes 49156 | tf_op jit(solution)/shard_map/dynamic_update_slice | solution.py:22
  258.8 1.6 copy.577
  260.4 4.1 %dynamic_update_slice.29 = bf16[12,128,64]{1,2,0:T(8,128)(2,1)S(1)} dynamic-update-slice(bf16[12,128,64]{1,2,0:T(8,128)(2,1)S(1)} %dynamic_update_slice.28, bf16[12,16,64]{1,2,0:T(8,128)(2,1)} %copy.577, s32[]{:T(128)} %constant.140.clone.1, s32[]{:T(128)S(6)} %select_n.243, s32[]{:T(128)} %constant.140.clone.1) | dynamic-update-slice | bytes 49156 | tf_op jit(solution)/shard_map/dynamic_update_slice | solution.py:22
  264.5 1.6 copy.578
  266.1 4.1 %dynamic_update_slice.30 = bf16[12,128,64]{1,2,0:T(8,128)(2,1)S(1)} dynamic-update-slice(bf16[12,128,64]{1,2,0:T(8,128)(2,1)S(1)} %dynamic_update_slice.29, bf16[12,16,64]{1,2,0:T(8,128)(2,1)} %copy.578, s32[]{:T(128)} %constant.140.clone.1, s32[]{:T(128)S(6)} %select_n.245, s32[]{:T(128)} %constant.140.clone.1) | dynamic-update-slice | bytes 49156 | tf_op jit(solution)/shard_map/dynamic_update_slice | solution.py:22
  270.2 1.6 copy.579
  271.8 4.1 %dynamic_update_slice.31 = bf16[12,128,64]{1,2,0:T(8,128)(2,1)S(1)} dynamic-update-slice(bf16[12,128,64]{1,2,0:T(8,128)(2,1)S(1)} %dynamic_update_slice.30, bf16[12,16,64]{1,2,0:T(8,128)(2,1)} %copy.579, s32[]{:T(128)} %constant.140.clone.1, s32[]{:T(128)S(6)} %select_n.247, s32[]{:T(128)} %constant.140.clone.1) | dynamic-update-slice | bytes 49156 | tf_op jit(solution)/shard_map/dynamic_update_slice | solution.py:22
  277.5 2.7 copy.580
  280.2 2.8 fusion.78
  284.9 2.1 fusion.40
  288.5 2.7 copy.548
  291.3 3.3 %fusion.26 = bf16[12,256,64]{1,2,0:T(8,128)(2,1)} fusion(bf16[12,256,64]{1,2,0:T(8,128)(2,1)} %bitcast.415, f32[12,256,256]{1,2,0:T(8,128)S(1)} %get-tuple-element.49, f32[12,256]{1,0:T(8,128)} %broadcast_maximum_fusion, pred[256]{0:T(512)(128)(4,1)} %add_compare_fusion.2, f32[12,256,64]{1,2,0:T(8,128)} %copy.580, f32[12,256,64]{1,2,0:T(8,128)} %copy.548, ...), kind=kOutput, calls=%fused_computation.23 | convolution fusion | flops 106561536 | bytes 5572864 | tf_op jit(solution)/shard_map/hqk,hke->hqe/dot_general | solution.py:79
  294.6 2.7 fusion.17
  (287 shorter events, 106.5 us)
Async XLA Ops:
  6.5 74.5 %all-gather.3.cloned.1.call-start = ((), (), s32[]{:S(2)}) async-start(), calls=%async_computation | async-start | bytes 4423680 | tf_op jit(solution)/shard_map/all_gather | solution.py:120
  7.3 287.4 %all-gather.5.cloned.1.call-start = ((), (), s32[]{:S(2)}) async-start(), calls=%async_computation.1 | async-start | bytes 1474560 | tf_op jit(solution)/shard_map/all_gather | solution.py:121
  94.5 151.1 %collective-permute-start = (bf16[12,64,64]{2,1,0:T(8,128)(2,1)}, bf16[12,64,64]{2,1,0:T(8,128)(2,1)}, u32[]{:S(2)}, u32[]{:S(2)}) collective-permute-start(bf16[12,64,64]{2,1,0:T(8,128)(2,1)} %constant_dynamic-update-slice_fusion.12), channel_id=1, source_target_pairs={{0,4},{4,0},{8,12},{12,8},{16,20},{20,16},{24,28},{28,24},{1,5},{5... | collective-permute-start | bytes 294920 | tf_op jit(solution)/shard_map/ppermute | solution.py:37
  95.4 28.1 %copy-start.1 = (bf16[256,768]{0,1:T(8,128)(2,1)}, bf16[256,768]{0,1:T(8,128)(2,1)S(1)}, u32[]{:S(2)}) copy-start(bf16[256,768]{0,1:T(8,128)(2,1)S(1)} %copy.419) | copy-start | bytes 1179652
  127.6 74.9 %copy-start.2 = (bf16[256,768]{0,1:T(8,128)(2,1)}, bf16[256,768]{0,1:T(8,128)(2,1)S(1)}, u32[]{:S(2)}) copy-start(bf16[256,768]{0,1:T(8,128)(2,1)S(1)} %copy.520) | copy-start | bytes 1179652
  161.0 41.6 %copy-start.7 = (bf16[64,1,64]{2,1,0:T(2,128)(2,1)S(1)}, bf16[64,1,64]{2,1,0:T(2,128)(2,1)}, u32[]{:S(2)}) copy-start(bf16[64,1,64]{2,1,0:T(2,128)(2,1)} %slice.558) | copy-start | bytes 24580
  161.0 42.2 %copy-start.8 = (bf16[64,1,64]{2,1,0:T(2,128)(2,1)S(1)}, bf16[64,1,64]{2,1,0:T(2,128)(2,1)}, u32[]{:S(2)}) copy-start(bf16[64,1,64]{2,1,0:T(2,128)(2,1)} %slice.560) | copy-start | bytes 24580
  161.0 42.8 %copy-start.9 = (bf16[64,1,64]{2,1,0:T(2,128)(2,1)S(1)}, bf16[64,1,64]{2,1,0:T(2,128)(2,1)}, u32[]{:S(2)}) copy-start(bf16[64,1,64]{2,1,0:T(2,128)(2,1)} %slice.562) | copy-start | bytes 24580
  161.0 43.4 %copy-start.10 = (bf16[64,1,64]{2,1,0:T(2,128)(2,1)S(1)}, bf16[64,1,64]{2,1,0:T(2,128)(2,1)}, u32[]{:S(2)}) copy-start(bf16[64,1,64]{2,1,0:T(2,128)(2,1)} %slice.564) | copy-start | bytes 24580
  161.0 44.0 %copy-start.11 = (bf16[64,1,64]{2,1,0:T(2,128)(2,1)S(1)}, bf16[64,1,64]{2,1,0:T(2,128)(2,1)}, u32[]{:S(2)}) copy-start(bf16[64,1,64]{2,1,0:T(2,128)(2,1)} %slice.566) | copy-start | bytes 24580
  161.0 44.6 %copy-start.12 = (bf16[64,1,64]{2,1,0:T(2,128)(2,1)S(1)}, bf16[64,1,64]{2,1,0:T(2,128)(2,1)}, u32[]{:S(2)}) copy-start(bf16[64,1,64]{2,1,0:T(2,128)(2,1)} %slice.568) | copy-start | bytes 24580
  161.0 45.2 %copy-start.13 = (bf16[64,1,64]{2,1,0:T(2,128)(2,1)S(1)}, bf16[64,1,64]{2,1,0:T(2,128)(2,1)}, u32[]{:S(2)}) copy-start(bf16[64,1,64]{2,1,0:T(2,128)(2,1)} %slice.570) | copy-start | bytes 24580
  161.0 45.8 %copy-start.14 = (bf16[64,1,64]{2,1,0:T(2,128)(2,1)S(1)}, bf16[64,1,64]{2,1,0:T(2,128)(2,1)}, u32[]{:S(2)}) copy-start(bf16[64,1,64]{2,1,0:T(2,128)(2,1)} %slice.572) | copy-start | bytes 24580
  161.0 46.4 %copy-start.3 = (bf16[12,128,64]{2,1,0:T(8,128)(2,1)S(1)}, bf16[12,128,64]{2,1,0:T(8,128)(2,1)}, u32[]{:S(2)}) copy-start(bf16[12,128,64]{2,1,0:T(8,128)(2,1)} %all_gather.10) | copy-start | bytes 589828
  161.0 46.4 %copy-start.21 = (pred[12,128]{1,0:T(8,128)(4,1)S(1)}, pred[12,128]{1,0:T(8,128)(4,1)}, u32[]{:S(2)}) copy-start(pred[12,128]{1,0:T(8,128)(4,1)} %add_compare_fusion.1) | copy-start | bytes 4612
  161.0 46.8 %copy-start.6 = (bf16[64,1,64]{2,1,0:T(2,128)(2,1)S(1)}, bf16[64,1,64]{2,1,0:T(2,128)(2,1)}, u32[]{:S(2)}) copy-start(bf16[64,1,64]{2,1,0:T(2,128)(2,1)} %slice.574) | copy-start | bytes 24580
  161.0 47.4 %copy-start.5 = (bf16[1,256,64]{2,1,0:T(8,128)(2,1)S(1)}, bf16[1,256,64]{2,1,0:T(8,128)(2,1)}, u32[]{:S(2)}) copy-start(bf16[1,256,64]{2,1,0:T(8,128)(2,1)} %copy.543) | copy-start | bytes 98308
  161.1 48.4 %copy-start.4 = (bf16[1,256,64]{2,1,0:T(8,128)(2,1)S(1)}, bf16[1,256,64]{2,1,0:T(8,128)(2,1)}, u32[]{:S(2)}) copy-start(bf16[1,256,64]{2,1,0:T(8,128)(2,1)} %copy.545) | copy-start | bytes 98308
  170.6 45.4 %copy-start.17 = (bf16[12,16,64]{2,1,0:T(8,128)(2,1)}, bf16[12,16,64]{2,1,0:T(8,128)(2,1)S(1)}, u32[]{:S(2)}) copy-start(bf16[12,16,64]{2,1,0:T(8,128)(2,1)S(1)} %constant_dynamic-update-slice_fusion.60) | copy-start | bytes 73732
  170.6 37.9 %collective-permute-start.4 = (bf16[12,16,64]{2,1,0:T(8,128)(2,1)S(1)}, bf16[12,16,64]{2,1,0:T(8,128)(2,1)S(1)}, u32[]{:S(2)}, u32[]{:S(2)}) collective-permute-start(bf16[12,16,64]{2,1,0:T(8,128)(2,1)S(1)} %constant_dynamic-update-slice_fusion.60), channel_id=1, source_target_pairs={{0,4},{4,8},{8,12},{12,16},{16,20},{20,24},{24,28},{28,0},{1,5},{5... | collective-permute-start | bytes 73736 | tf_op jit(solution)/shard_map/ppermute | solution.py:21
  200.4 7.0 %copy-start.16 = (bf16[12,16,64]{2,1,0:T(8,128)(2,1)S(1)}, bf16[12,16,64]{2,1,0:T(8,128)(2,1)}, u32[]{:S(2)}) copy-start(bf16[12,16,64]{2,1,0:T(8,128)(2,1)} %constant_dynamic-update-slice_fusion.24) | copy-start | bytes 73732
  208.5 7.5 %copy-start.18 = (bf16[12,16,64]{2,1,0:T(8,128)(2,1)}, bf16[12,16,64]{2,1,0:T(8,128)(2,1)S(1)}, u32[]{:S(2)}) copy-start(bf16[12,16,64]{2,1,0:T(8,128)(2,1)S(1)} %collective-permute-done.4) | copy-start | bytes 73732
  208.5 1.6 collective-permute-start.5
  210.1 9.6 %copy-start.19 = (bf16[12,16,64]{2,1,0:T(8,128)(2,1)}, bf16[12,16,64]{2,1,0:T(8,128)(2,1)S(1)}, u32[]{:S(2)}) copy-start(bf16[12,16,64]{2,1,0:T(8,128)(2,1)S(1)} %collective-permute-done.5) | copy-start | bytes 73732
  210.1 3.5 %collective-permute-start.6 = (bf16[12,16,64]{2,1,0:T(8,128)(2,1)S(1)}, bf16[12,16,64]{2,1,0:T(8,128)(2,1)S(1)}, u32[]{:S(2)}, u32[]{:S(2)}) collective-permute-start(bf16[12,16,64]{2,1,0:T(8,128)(2,1)S(1)} %collective-permute-done.5), channel_id=1, source_target_pairs={{0,4},{4,8},{8,12},{12,16},{16,20},{20,24},{24,28},{28,0},{1,5},{5... | collective-permute-start | bytes 73736 | tf_op jit(solution)/shard_map/ppermute | solution.py:21
  213.6 6.1 %copy-start.20 = (bf16[12,16,64]{2,1,0:T(8,128)(2,1)}, bf16[12,16,64]{2,1,0:T(8,128)(2,1)S(1)}, u32[]{:S(2)}) copy-start(bf16[12,16,64]{2,1,0:T(8,128)(2,1)S(1)} %collective-permute-done.6) | copy-start | bytes 73732
  213.6 4.4 %collective-permute-start.7 = (bf16[12,16,64]{2,1,0:T(8,128)(2,1)S(1)}, bf16[12,16,64]{2,1,0:T(8,128)(2,1)S(1)}, u32[]{:S(2)}, u32[]{:S(2)}) collective-permute-start(bf16[12,16,64]{2,1,0:T(8,128)(2,1)S(1)} %collective-permute-done.6), channel_id=1, source_target_pairs={{0,4},{4,8},{8,12},{12,16},{16,20},{20,24},{24,28},{28,0},{1,5},{5... | collective-permute-start | bytes 73736 | tf_op jit(solution)/shard_map/ppermute | solution.py:21
  218.0 25.6 %collective-permute-start.8 = (bf16[12,16,64]{2,1,0:T(8,128)(2,1)S(1)}, bf16[12,16,64]{2,1,0:T(8,128)(2,1)}, u32[]{:S(2)}, u32[]{:S(2)}) collective-permute-start(bf16[12,16,64]{2,1,0:T(8,128)(2,1)S(1)} %collective-permute-done.7), channel_id=1, source_target_pairs={{0,4},{4,8},{8,12},{12,16},{16,20},{20,24},{24,28},{28,0},{1,5},{5... | collective-permute-start | bytes 73736 | tf_op jit(solution)/shard_map/ppermute | solution.py:21
  221.6 27.9 %collective-permute-start.2 = (bf16[12,64,64]{2,1,0:T(8,128)(2,1)}, bf16[12,64,64]{2,1,0:T(8,128)(2,1)}, u32[]{:S(2)}, u32[]{:S(2)}) collective-permute-start(bf16[12,64,64]{2,1,0:T(8,128)(2,1)} %constant_dynamic-update-slice_fusion.48), channel_id=1, source_target_pairs={{0,4},{4,0},{8,12},{12,8},{16,20},{20,16},{24,28},{28,24},{1,5},{5... | collective-permute-start | bytes 294920 | tf_op jit(solution)/shard_map/ppermute | solution.py:37
  223.9 52.0 %copy-start.22 = (pred[12,128]{1,0:T(8,128)(4,1)S(1)}, pred[12,128]{1,0:T(8,128)(4,1)}, u32[]{:S(2)}) copy-start(pred[12,128]{1,0:T(8,128)(4,1)} %add_compare_fusion.1) | copy-start | bytes 4612
  243.6 5.5 %collective-permute-start.9 = (bf16[12,16,64]{2,1,0:T(8,128)(2,1)}, bf16[12,16,64]{2,1,0:T(8,128)(2,1)}, u32[]{:S(2)}, u32[]{:S(2)}) collective-permute-start(bf16[12,16,64]{2,1,0:T(8,128)(2,1)} %collective-permute-done.8), channel_id=1, source_target_pairs={{0,4},{4,8},{8,12},{12,16},{16,20},{20,24},{24,28},{28,0},{1,5},{5... | collective-permute-start | bytes 73736 | tf_op jit(solution)/shard_map/ppermute | solution.py:21
  247.8 32.4 %collective-permute-start.1 = (bf16[12,128,64]{2,1,0:T(8,128)(2,1)}, bf16[12,128,64]{2,1,0:T(8,128)(2,1)}, u32[]{:S(2)}, u32[]{:S(2)}) collective-permute-start(bf16[12,128,64]{2,1,0:T(8,128)(2,1)} %maximum_select_fusion.4), channel_id=1, source_target_pairs={{0,8},{4,12},{8,0},{12,4},{16,24},{20,28},{24,16},{28,20},{1,9},{5... | collective-permute-start | bytes 589832 | tf_op jit(solution)/shard_map/ppermute | solution.py:37
  249.0 21.2 %collective-permute-start.10 = (bf16[12,16,64]{2,1,0:T(8,128)(2,1)}, bf16[12,16,64]{2,1,0:T(8,128)(2,1)}, u32[]{:S(2)}, u32[]{:S(2)}) collective-permute-start(bf16[12,16,64]{2,1,0:T(8,128)(2,1)} %collective-permute-done.9), channel_id=1, source_target_pairs={{0,4},{4,8},{8,12},{12,16},{16,20},{20,24},{24,28},{28,0},{1,5},{5... | collective-permute-start | bytes 73736 | tf_op jit(solution)/shard_map/ppermute | solution.py:21
  251.6 33.2 %collective-permute-start.3 = (bf16[12,128,64]{2,1,0:T(8,128)(2,1)}, bf16[12,128,64]{2,1,0:T(8,128)(2,1)}, u32[]{:S(2)}, u32[]{:S(2)}) collective-permute-start(bf16[12,128,64]{2,1,0:T(8,128)(2,1)} %maximum_select_fusion.5), channel_id=1, source_target_pairs={{0,8},{4,12},{8,0},{12,4},{16,24},{20,28},{24,16},{28,20},{1,9},{5... | collective-permute-start | bytes 589832 | tf_op jit(solution)/shard_map/ppermute | solution.py:37
  258.8 21.4 %copy-start.23 = (pred[12,256]{1,0:T(8,128)(4,1)S(1)}, pred[12,256]{1,0:T(8,128)(4,1)}, u32[]{:S(2)}) copy-start(pred[12,256]{1,0:T(8,128)(4,1)} %add_compare_fusion) | copy-start | bytes 9220
  276.2 4.0 %copy-start.26 = (bf16[12,64,64]{2,1,0:T(8,128)(2,1)S(1)}, bf16[12,64,64]{2,1,0:T(8,128)(2,1)}, u32[]{:S(2)}) copy-start(bf16[12,64,64]{2,1,0:T(8,128)(2,1)} %constant_dynamic-update-slice_fusion) | copy-start | bytes 294916
  287.0 4.2 %copy-start.15 = (f32[12,256]{1,0:T(8,128)S(1)}, f32[12,256]{1,0:T(8,128)}, u32[]{:S(2)}) copy-start(f32[12,256]{1,0:T(8,128)} %fusion.1) | copy-start | bytes 36868
  287.0 4.2 %copy-start.24 = (pred[12,256]{1,0:T(8,128)(4,1)S(1)}, pred[12,256]{1,0:T(8,128)(4,1)}, u32[]{:S(2)}) copy-start(pred[12,256]{1,0:T(8,128)(4,1)} %copy.470) | copy-start | bytes 9220
  287.0 4.2 %copy-start.25 = (pred[12,256]{1,0:T(8,128)(4,1)S(1)}, pred[12,256]{1,0:T(8,128)(4,1)}, u32[]{:S(2)}) copy-start(pred[12,256]{1,0:T(8,128)(4,1)} %broadcast_in_dim.264) | copy-start | bytes 9220
  291.3 3.4 %copy-start = (bf16[1,256,768]{2,1,0:T(8,128)(2,1)S(1)}, bf16[1,256,768]{2,1,0:T(8,128)(2,1)}, u32[]{:S(2)}) copy-start(bf16[1,256,768]{2,1,0:T(8,128)(2,1)} %param.6) | copy-start | bytes 1179652
Sparse Core Ops, SparseCore 0:
  8.9 72.0 all-gather.2
  82.6 28.4 all-gather.4
